TPU v7x, 256 devices: a whole 4x4x8 slice. The times are simulated.
256 devices in a mesh: dp: 32 (over z, y), tensor: 8 (over x, core).
Axes of the slice: x: 4, y: 4, z: 8, core: 2. Of those that a mesh axis runs over, the one named last changes fastest.
Arguments:
- hidden: bfloat16 [4096, 26624], P('dp', 'tensor'), may hold values from -6 to 6
- out_grad: bfloat16 [4096, 8192], P(('dp', 'tensor')), may hold values from -0.375 to 0.375
- master: float32 [8192, 26624], P('dp', 'tensor'), may hold values from -0.3125 to 0.3125
- first_moment: bfloat16 [8192, 26624], P('dp', 'tensor'), may hold values from -4 to 4
- second_moment: bfloat16 [8192, 26624], P('dp', 'tensor'), may hold values from 0.049804688 to 1
- row_counts: int32 [8], replicated, may hold values from 2816 to 3840, as said below
- step_count: int32 [1], replicated, may hold values from 1 to 11
Outputs:
- adam_update: float32 [8192, 26624], P('dp', 'tensor')
- weights_tp: bfloat16 [8192, 30720], P('dp', 'tensor')
Inputs may be any that keep to these rules, and one draw needn't show every extreme that they name: Tensor index j takes row_counts[j] consecutive hidden units in order; they sum to 26624; offsets[j] differs from j * 3328 by at most 256; the largest count equals 3840.
All inputs are finite; a program needn't handle non-finite values.
Results may differ from a plain program's by a relative error of at most 0.0045.
Values may be sent and summed in bfloat16 or wider, within the bound.
No kernel may reach another device: no remote copies, remote signals or barrier semaphores. Data moves between devices by JAX's collectives and lax.ppermute only.
A program may use at most 192 MiB of HBM per device.

v0:
```python
import jax
import jax.numpy as jnp
import numpy as np
from jax import lax
from jax.sharding import Mesh, PartitionSpec as P

DRIFT = 256
CAP = 3840
CHUNKS = ((0, 896), (2432, 3328), (896, 1664), (1664, 2432))
beta_first = 0.9
beta_second = 0.95
epsilon = 1e-08
decay_rate = 0.1
learn_rate = 0.001
TENSOR = ("x", "core")


def adamw(gradient, master, first_moment, second_moment, first_fix, second_fix):
    first_new = beta_first * first_moment + (1.0 - beta_first) * gradient
    second_new = beta_second * second_moment + (1.0 - beta_second) * gradient * gradient
    update = (
        first_new / first_fix / (jnp.sqrt(second_new / second_fix) + epsilon) + decay_rate * master
    )
    master_new = master - learn_rate * update
    return (master_new, update)


def per_device(hidden, out_grad, master, first_moment, second_moment, row_counts, step_count):
    width = hidden.shape[1]
    tensor_count = lax.axis_size(TENSOR)
    z_count = lax.axis_size("z")
    local_tokens = out_grad.shape[0]
    features = out_grad.shape[1] // z_count
    regrouped = lax.all_to_all(out_grad, "z", split_axis=1, concat_axis=0, tiled=True)
    spread = lax.all_gather(regrouped, TENSOR, axis=0, tiled=True)
    cotangent = spread.reshape(tensor_count, z_count, local_tokens, features)
    cotangent = cotangent.transpose(1, 0, 2, 3).reshape(-1, features)
    steps_done = step_count[0].astype(jnp.float32)
    first_fix = 1.0 - jnp.power(beta_first, steps_done)
    second_fix = 1.0 - jnp.power(beta_second, steps_done)
    gathered = [
        lax.all_gather(hidden[:, low:high], "z", axis=0, tiled=True) for low, high in CHUNKS
    ]
    updates = {}
    weights = {}
    for (low, high), acts in zip(CHUNKS, gathered):
        partial_value = lax.dot_general(
            cotangent, acts, (((0,), (0,)), ((), ())), preferred_element_type=jnp.float32
        ).astype(jnp.bfloat16)
        gradient = lax.psum_scatter(partial_value, "y", scatter_dimension=0, tiled=True)
        master_new, update = adamw(
            gradient.astype(jnp.float32),
            master[:, low:high],
            first_moment[:, low:high].astype(jnp.float32),
            second_moment[:, low:high].astype(jnp.float32),
            first_fix,
            second_fix,
        )
        updates[low] = update
        weights[low] = master_new.astype(jnp.bfloat16)
    order = sorted(updates)
    head = weights[order[0]][:, :DRIFT]
    tail = weights[order[-1]][:, -DRIFT:]
    ends = tensor_count - 1
    left = lax.ppermute(tail, TENSOR, [(i, i + 1) for i in range(ends)])
    right = lax.ppermute(head, TENSOR, [(i + 1, i) for i in range(ends)])
    position = lax.axis_index(TENSOR)
    places = jnp.arange(tensor_count, dtype=jnp.int32)
    first_slot = jnp.sum(jnp.where(places < position, row_counts, 0))
    length = jnp.sum(jnp.where(places == position, row_counts, 0))
    rows = master.shape[0]
    widened = jnp.concatenate(
        [left] + [weights[k] for k in order] + [right, jnp.zeros((rows, 2 * DRIFT), jnp.bfloat16)],
        axis=1,
    )
    start = first_slot - position * width + DRIFT
    window = lax.dynamic_slice_in_dim(widened, start, CAP, 1)
    slot_index = jnp.arange(CAP, dtype=jnp.int32)
    laid = jnp.where((slot_index < length)[None, :], window, jnp.zeros((), jnp.bfloat16))
    return (jnp.concatenate([updates[k] for k in order], axis=1), laid)


def solution(mesh):
    fine = Mesh(np.asarray(mesh.devices).reshape(8, 4, 4, 2), ("z", "y", "x", "core"))
    dp = ("z", "y")
    return jax.shard_map(
        per_device,
        mesh=fine,
        in_specs=(
            P(dp, TENSOR),
            P(dp + TENSOR, None),
            P(dp, TENSOR),
            P(dp, TENSOR),
            P(dp, TENSOR),
            P(),
            P(),
        ),
        out_specs=(P(dp, TENSOR), P(dp, TENSOR)),
        check_vma=False,
    )
```

profile of v0, /device:TPU:2, one launch (start us, length us, event | category | flops | bytes accessed | tf_op | source)
XLA Modules:
  0.0 358.5 jit_solution(4531047940108893145)
XLA Ops:
  8.2 20.2 %all_to_all.19 = bf16[16,8,1024]{2,0,1:T(8,128)(2,1)} all-to-all(bf16[16,8,1024]{2,0,1:T(8,128)(2,1)S(1)} %bitcast.27), channel_id=1, replica_groups=mesh['z'=8,'y'=4,'x'=4,'core'=2] {'z'}, dimensions={1} | all-to-all | bytes 524288 | tf_op jit(solution)/shard_map/all_to_all | solution.py:34
  28.5 1.9 fusion.41
  33.6 18.1 %all-gather.6.cloned.1.call-done = bf16[1024,1024]{1,0:T(8,128)(2,1)} async-done(((bf16[128,1024]{1,0:T(8,128)(2,1)}), bf16[1024,1024]{1,0:T(8,128)(2,1)}) %all-gather.6.cloned.1.call-update) | async-done | bytes 2097168 | tf_op jit(solution)/shard_map/all_gather | solution.py:35
  53.5 42.4 %all-gather.14.cloned.1.call-done = bf16[1024,896]{1,0:T(8,128)(2,1)} async-done(((bf16[128,896]{1,0:T(8,128)(2,1)}), bf16[1024,896]{1,0:T(8,128)(2,1)}) %all-gather.14.cloned.1.call-update) | async-done | bytes 1835024 | tf_op jit(solution)/shard_map/all_gather | solution.py:42
  95.9 5.1 %convolution_convert_fusion = bf16[1024,896]{1,0:T(8,128)(2,1)} fusion(bf16[1024,1024]{1,0:T(8,128)(2,1)S(1)} %bitcast.22, bf16[1024,896]{1,0:T(8,128)(2,1)} %all-gather.14.cloned.1.call-done), kind=kOutput, calls=%fused_computation.2 | convolution fusion | flops 1879965696 | bytes 5767168 | tf_op jit(solution)/shard_map/dot_general | solution.py:47
  101.1 36.4 %all-gather.8.cloned.1.call-done = bf16[1024,896]{1,0:T(8,128)(2,1)} async-done(((bf16[128,896]{1,0:T(8,128)(2,1)}), bf16[1024,896]{1,0:T(8,128)(2,1)}) %all-gather.8.cloned.1.call-update) | async-done | bytes 1835024 | tf_op jit(solution)/shard_map/all_gather | solution.py:42
  137.5 5.1 %convolution_convert_fusion.1 = bf16[1024,896]{1,0:T(8,128)(2,1)} fusion(bf16[1024,1024]{1,0:T(8,128)(2,1)S(1)} %bitcast.23, bf16[1024,896]{1,0:T(8,128)(2,1)} %all-gather.8.cloned.1.call-done), kind=kOutput, calls=%fused_computation.3 | convolution fusion | flops 1879965696 | bytes 5767168 | tf_op jit(solution)/shard_map/dot_general | solution.py:47
  142.7 35.1 %all-gather.10.cloned.1.call-done = bf16[1024,768]{1,0:T(8,128)(2,1)} async-done(((bf16[128,768]{1,0:T(8,128)(2,1)}), bf16[1024,768]{1,0:T(8,128)(2,1)}) %all-gather.10.cloned.1.call-update) | async-done | bytes 1572880 | tf_op jit(solution)/shard_map/all_gather | solution.py:42
  177.7 4.4 %convolution_convert_fusion.3 = bf16[1024,768]{1,0:T(8,128)(2,1)} fusion(bf16[1024,1024]{1,0:T(8,128)(2,1)S(1)} %bitcast.24, bf16[1024,768]{1,0:T(8,128)(2,1)} %all-gather.10.cloned.1.call-done), kind=kOutput, calls=%fused_computation.5 | convolution fusion | flops 1611399168 | bytes 5242880 | tf_op jit(solution)/shard_map/dot_general | solution.py:47
  182.2 35.8 %all-gather.12.cloned.1.call-done = bf16[1024,768]{1,0:T(8,128)(2,1)} async-done(((bf16[128,768]{1,0:T(8,128)(2,1)}), bf16[1024,768]{1,0:T(8,128)(2,1)}) %all-gather.12.cloned.1.call-update) | async-done | bytes 1572880 | tf_op jit(solution)/shard_map/all_gather | solution.py:42
  218.0 4.4 %convolution_convert_fusion.2 = bf16[1024,768]{1,0:T(8,128)(2,1)} fusion(bf16[1024,1024]{1,0:T(8,128)(2,1)S(1)} %bitcast.25, bf16[1024,768]{1,0:T(8,128)(2,1)} %all-gather.12.cloned.1.call-done), kind=kOutput, calls=%fused_computation.4 | convolution fusion | flops 1611399168 | bytes 5242880 | tf_op jit(solution)/shard_map/dot_general | solution.py:47
  223.2 26.5 %reduce-scatter.11.cloned.1.call-done = bf16[256,896]{1,0:T(8,128)(2,1)} async-done(((bf16[1024,896]{1,0:T(8,128)(2,1)}), bf16[256,896]{1,0:T(8,128)(2,1)}) %reduce-scatter.11.cloned.1.call-update) | async-done | bytes 458768 | tf_op jit(solution)/shard_map/reduce_scatter | solution.py:50
  249.8 2.4 subtract_convert_fusion.1
  252.1 1.9 collective-permute-start
  256.0 2.5 collective-permute-done
  259.1 23.7 %reduce-scatter.5.cloned.1.call-done = bf16[256,896]{1,0:T(8,128)(2,1)} async-done(((bf16[1024,896]{1,0:T(8,128)(2,1)}), bf16[256,896]{1,0:T(8,128)(2,1)}) %reduce-scatter.5.cloned.1.call-update) | async-done | bytes 458768 | tf_op jit(solution)/shard_map/reduce_scatter | solution.py:50
  282.8 3.2 constant_dynamic-update-slice_fusion.2
  286.0 2.1 collective-permute-start.1
  288.2 25.2 %reduce-scatter.7.cloned.1.call-done = bf16[256,768]{1,0:T(8,128)(2,1)} async-done(((bf16[1024,768]{1,0:T(8,128)(2,1)}), bf16[256,768]{1,0:T(8,128)(2,1)}) %reduce-scatter.7.cloned.1.call-update) | async-done | bytes 393232 | tf_op jit(solution)/shard_map/reduce_scatter | solution.py:50
  313.3 3.0 fusion.32
  316.3 27.6 %reduce-scatter.9.cloned.1.call-done = bf16[256,768]{1,0:T(8,128)(2,1)} async-done(((bf16[1024,768]{1,0:T(8,128)(2,1)}), bf16[256,768]{1,0:T(8,128)(2,1)}) %reduce-scatter.9.cloned.1.call-update) | async-done | bytes 393232 | tf_op jit(solution)/shard_map/reduce_scatter | solution.py:50
  343.9 2.9 fusion.33
  346.9 2.0 pad_maximum_fusion
  349.7 2.4 dynamic-slice_select_fusion
  (34 shorter events, 9.0 us)
Async XLA Ops:
  7.2 44.6 %all-gather.6.cloned.1.call-start = ((), (), s32[]{:S(2)}) async-start(), calls=%async_computation.5 | async-start | bytes 2359296 | tf_op jit(solution)/shard_map/all_gather | solution.py:35
  28.5 67.5 %all-gather.14.cloned.1.call-start = ((), (), s32[]{:S(2)}) async-start(), calls=%async_computation.12 | async-start | bytes 2064384 | tf_op jit(solution)/shard_map/all_gather | solution.py:42
  30.4 107.1 %all-gather.8.cloned.1.call-start = ((), (), s32[]{:S(2)}) async-start(), calls=%async_computation.6 | async-start | bytes 2064384 | tf_op jit(solution)/shard_map/all_gather | solution.py:42
  31.1 146.6 %all-gather.10.cloned.1.call-start = ((), (), s32[]{:S(2)}) async-start(), calls=%async_computation.8 | async-start | bytes 1769472 | tf_op jit(solution)/shard_map/all_gather | solution.py:42
  33.0 185.0 %all-gather.12.cloned.1.call-start = ((), (), s32[]{:S(2)}) async-start(), calls=%async_computation.10 | async-start | bytes 1769472 | tf_op jit(solution)/shard_map/all_gather | solution.py:42
  33.6 216.2 %reduce-scatter.11.cloned.1.call-start = ((), (), s32[]{:S(2)}) async-start(), calls=%async_computation.13 | async-start | bytes 2293760 | tf_op jit(solution)/shard_map/reduce_scatter | solution.py:50
  101.1 181.7 %reduce-scatter.5.cloned.1.call-start = ((), (), s32[]{:S(2)}) async-start(), calls=%async_computation.7 | async-start | bytes 2293760 | tf_op jit(solution)/shard_map/reduce_scatter | solution.py:50
  142.6 170.7 %reduce-scatter.7.cloned.1.call-start = ((), (), s32[]{:S(2)}) async-start(), calls=%async_computation.9 | async-start | bytes 1966080 | tf_op jit(solution)/shard_map/reduce_scatter | solution.py:50
  182.2 161.8 %reduce-scatter.9.cloned.1.call-start = ((), (), s32[]{:S(2)}) async-start(), calls=%async_computation.11 | async-start | bytes 1966080 | tf_op jit(solution)/shard_map/reduce_scatter | solution.py:50
  222.5 31.6 %copy-start.1 = (s32[8]{0:T(128)S(1)}, s32[8]{0:T(128)}, u32[]{:S(2)}) copy-start(s32[8]{0:T(128)} %param.12) | copy-start | bytes 100
  252.1 6.3 %collective-permute-start = (bf16[256,256]{1,0:T(8,128)(2,1)S(1)}, bf16[256,256]{1,0:T(8,128)(2,1)S(1)}, u32[]{:S(2)}, u32[]{:S(2)}) collective-permute-start(bf16[256,256]{1,0:T(8,128)(2,1)S(1)} %slice.72), channel_id=1, source_target_pairs={{0,1},{1,2},{2,3},{3,4},{4,5},{5,6},{6,7},{8,9},{9,10},{10,11},{11... | collective-permute-start | bytes 393224 | tf_op jit(solution)/shard_map/ppermute | solution.py:65
  286.0 63.6 %collective-permute-start.1 = (bf16[256,256]{1,0:T(8,128)(2,1)S(1)}, bf16[256,256]{1,0:T(8,128)(2,1)S(1)}, u32[]{:S(2)}, u32[]{:S(2)}) collective-permute-start(bf16[256,256]{1,0:T(8,128)(2,1)S(1)} %slice.73), channel_id=1, source_target_pairs={{1,0},{2,1},{3,2},{4,3},{5,4},{6,5},{7,6},{9,8},{10,9},{11,10},{12... | collective-permute-start | bytes 393224 | tf_op jit(solution)/shard_map/ppermute | solution.py:66
  346.9 2.7 copy-start
Sparse Core Ops, SparseCore 0:
  28.6 23.1 all-gather.5
  54.1 41.7 all-gather.13
  98.3 39.1 all-gather.7
  139.1 38.5 all-gather.9
  179.4 38.5 all-gather.11
  221.0 28.7 reduce-scatter.10
  252.9 29.8 reduce-scatter.4
  285.3 27.9 reduce-scatter.6
  315.9 27.9 reduce-scatter.8
where the time goes:
time: 359 us
  waiting for transfers between devices  275 us (77%)
  blocking collectives  20.2 us (6%)
  matrix products  19.1 us (5%)
  other arithmetic  17.1 us (5%)
  between operations  15.3 us (4%)
  local copies, waits for them, and re-layouts  7.9 us (2%)
  starting transfers between devices  4.42 us (1%)
    all_gather x4, waiting for transfers between devices, per_device(): lax.all_gather(hidden[:, low:high], 'z', axis=0, tiled=True)  150 us
    reduce_scatter x4, waiting for transfers between devices, per_device(): lax.psum_scatter(partial_value, 'y', scatter_dimension=0, tiled=True)  103 us
    all_to_all x1, blocking collectives, per_device(): lax.all_to_all(out_grad, 'z', split_axis=1, concat_axis=0, tiled=True)  20.2 us
    dot_general x4, matrix products, per_device(): lax.dot_general(cotangent, acts, (((0,), (0,)), ((), ())), preferred_elem...  19.1 us
    all_gather x1, waiting for transfers between devices, per_device(): spread = lax.all_gather(regrouped, TENSOR, axis=0, tiled=True)  18.1 us
    unnamed x3, other arithmetic  9.14 us
  transfers between devices with their start and end apart: 11, of which 10 were waited for; matrix products, arithmetic and copies ran while one was open for 11% of the time, Pallas kernels for 0%

commit v1 on v0

--- a/solution.py
+++ b/solution.py
@@ -39,7 +39,10 @@
     first_fix = 1.0 - jnp.power(beta_first, steps_done)
     second_fix = 1.0 - jnp.power(beta_second, steps_done)
     gathered = [
-        lax.all_gather(hidden[:, low:high], "z", axis=0, tiled=True) for low, high in CHUNKS
+        jnp.concatenate(
+            lax.all_to_all(jnp.stack([hidden[:, low:high]] * lax.axis_size("z")), "z", 0, 0), axis=0
+        )
+        for low, high in CHUNKS
     ]
     updates = {}
     weights = {}

time: 359 us -> 266 us (0.74)
  waiting for transfers between devices: 275 us -> 124 us
  blocking collectives: 20.2 us -> 62 us
  starting transfers between devices: 4.42 us -> 17.2 us
    all_gather x4 -> x0, waiting for transfers between devices: 150 us -> none  [per_device(): lax.all_gather(hidden[:, low:high], 'z', axis=0, tiled=True)]
    all_to_all x0 -> x3, waiting for transfers between devices: none -> 99.4 us  [per_device(): lax.all_to_all(jnp.stack([hidden[:, low:high]] * lax.axis_size('z')), 'z'...]
    reduce_scatter x4, waiting for transfers between devices: 103 us -> 6.52 us  [per_device(): lax.psum_scatter(partial_value, 'y', scatter_dimension=0, tiled=True)]
    all_to_all x0 -> x1, blocking collectives: none -> 41.7 us  [per_device(): lax.all_to_all(jnp.stack([hidden[:, low:high]] * lax.axis_size('z')), 'z'...]
    all_to_all x0 -> x3, starting transfers between devices: none -> 12.9 us  [per_device(): lax.all_to_all(jnp.stack([hidden[:, low:high]] * lax.axis_size('z')), 'z'...]
    another operation x0 -> x4, local copies, waits for them, and re-layouts: none -> 4.29 us  [per_device(): jnp.stack([hidden[:, low:high]] * lax.axis_size('z'))]
  transfers between devices with their start and end apart: 11 -> 10, of which waited for: 10 -> 6; matrix products, arithmetic and copies ran while one was open for 11% -> 16% of each run, Pallas kernels for 0% -> 0%
where the time goes in v1:
time: 266 us
  waiting for transfers between devices  124 us (47%)
  blocking collectives  62 us (23%)
  matrix products  19.1 us (7%)
  starting transfers between devices  17.2 us (6%)
  other arithmetic  17.1 us (6%)
  between operations  15.3 us (6%)
  local copies, waits for them, and re-layouts  10.7 us (4%)
    all_to_all x3, waiting for transfers between devices, per_device(): lax.all_to_all(jnp.stack([hidden[:, low:high]] * lax.axis_size('z')), 'z'...  99.4 us
    all_to_all x1, blocking collectives, per_device(): lax.all_to_all(jnp.stack([hidden[:, low:high]] * lax.axis_size('z')), 'z'...  41.7 us
    all_to_all x1, blocking collectives, per_device(): lax.all_to_all(out_grad, 'z', split_axis=1, concat_axis=0, tiled=True)  20.2 us
    dot_general x4, matrix products, per_device(): lax.dot_general(cotangent, acts, (((0,), (0,)), ((), ())), preferred_elem...  19.1 us
    all_gather x1, waiting for transfers between devices, per_device(): spread = lax.all_gather(regrouped, TENSOR, axis=0, tiled=True)  16 us
    all_to_all x3, starting transfers between devices, per_device(): lax.all_to_all(jnp.stack([hidden[:, low:high]] * lax.axis_size('z')), 'z'...  12.9 us
    unnamed x3, other arithmetic  9.12 us
    reduce_scatter x4, waiting for transfers between devices, per_device(): lax.psum_scatter(partial_value, 'y', scatter_dimension=0, tiled=True)  6.52 us
  transfers between devices with their start and end apart: 10, of which 6 were waited for; matrix products, arithmetic and copies ran while one was open for 16% of the time, Pallas kernels for 0%

profile of v1, /device:TPU:2, one launch (start us, length us, event | category | flops | bytes accessed | tf_op | source)
XLA Modules:
  0.0 265.6 jit_solution(1569552806116474736)
XLA Ops:
  8.2 20.2 %all_to_all.39 = bf16[16,8,1024]{2,0,1:T(8,128)(2,1)} all-to-all(bf16[16,8,1024]{2,0,1:T(8,128)(2,1)S(1)} %bitcast.32), channel_id=1, replica_groups=mesh['z'=8,'y'=4,'x'=4,'core'=2] {'z'}, dimensions={1} | all-to-all | bytes 524288 | tf_op jit(solution)/shard_map/all_to_all | solution.py:34
  31.0 4.3 %all-to-all-start.4 = ((bf16[8,128,896]{2,1,0:T(8,128)(2,1)}), bf16[8,128,896]{2,1,0:T(8,128)(2,1)}, u32[]{:S(2)}, u32[]{:S(2)}) async-start(bf16[8,128,896]{2,1,0:T(8,128)(2,1)} %stack.11), calls=%async_computation.7 | async-start | bytes 3670016 | tf_op jit(solution)/shard_map/all_to_all | solution.py:43
  35.3 16.0 %all-gather.2.cloned.1.call-done = bf16[1024,1024]{1,0:T(8,128)(2,1)} async-done(((bf16[128,1024]{1,0:T(8,128)(2,1)}), bf16[1024,1024]{1,0:T(8,128)(2,1)}) %all-gather.2.cloned.1.call-update) | async-done | bytes 2097168 | tf_op jit(solution)/shard_map/all_gather | solution.py:35
  51.4 1.8 copy.13
  53.2 26.2 %all-to-all-done.4 = bf16[8,128,896]{2,1,0:T(8,128)(2,1)} async-done(((bf16[8,128,896]{2,1,0:T(8,128)(2,1)}), bf16[8,128,896]{2,1,0:T(8,128)(2,1)}, u32[]{:S(2)}, u32[]{:S(2)}) %all-to-all-start.4) | async-done | bytes 1835040 | tf_op jit(solution)/shard_map/all_to_all | solution.py:43
  80.9 4.3 %all-to-all-start.1 = ((bf16[8,128,896]{2,1,0:T(8,128)(2,1)}), bf16[8,128,896]{2,1,0:T(8,128)(2,1)}, u32[]{:S(2)}, u32[]{:S(2)}) async-start(bf16[8,128,896]{2,1,0:T(8,128)(2,1)} %stack.8), calls=%async_computation.1 | async-start | bytes 3670016 | tf_op jit(solution)/shard_map/all_to_all | solution.py:43
  85.2 5.1 %convolution_convert_fusion = bf16[1024,896]{1,0:T(8,128)(2,1)} fusion(bf16[1024,1024]{1,0:T(8,128)(2,1)S(1)} %bitcast.25, bf16[1024,896]{1,0:T(8,128)(2,1)} %bitcast.11), kind=kOutput, calls=%fused_computation.2 | convolution fusion | flops 1879965696 | bytes 5767168 | tf_op jit(solution)/shard_map/dot_general | solution.py:50
  90.4 40.8 %all-to-all-done.1 = bf16[8,128,896]{2,1,0:T(8,128)(2,1)} async-done(((bf16[8,128,896]{2,1,0:T(8,128)(2,1)}), bf16[8,128,896]{2,1,0:T(8,128)(2,1)}, u32[]{:S(2)}, u32[]{:S(2)}) %all-to-all-start.1) | async-done | bytes 1835040 | tf_op jit(solution)/shard_map/all_to_all | solution.py:43
  131.2 5.1 %convolution_convert_fusion.1 = bf16[1024,896]{1,0:T(8,128)(2,1)} fusion(bf16[1024,1024]{1,0:T(8,128)(2,1)S(1)} %bitcast.26, bf16[1024,896]{1,0:T(8,128)(2,1)} %bitcast.5), kind=kOutput, calls=%fused_computation.3 | convolution fusion | flops 1879965696 | bytes 5767168 | tf_op jit(solution)/shard_map/dot_general | solution.py:50
  137.5 41.7 %all_to_all.40 = bf16[8,128,768]{2,1,0:T(8,128)(2,1)} all-to-all(bf16[8,128,768]{2,1,0:T(8,128)(2,1)S(1)} %stack.9), channel_id=1, replica_groups=mesh['z'=8,'y'=4,'x'=4,'core'=2] {'z'}, dimensions={0} | all-to-all | bytes 3145728 | tf_op jit(solution)/shard_map/all_to_all | solution.py:43
  180.5 4.3 %all-to-all-start.3 = ((bf16[8,128,768]{2,1,0:T(8,128)(2,1)}), bf16[8,128,768]{2,1,0:T(8,128)(2,1)}, u32[]{:S(2)}, u32[]{:S(2)}) async-start(bf16[8,128,768]{2,1,0:T(8,128)(2,1)} %stack.10), calls=%async_computation.5 | async-start | bytes 3145728 | tf_op jit(solution)/shard_map/all_to_all | solution.py:43
  184.9 4.4 %convolution_convert_fusion.3 = bf16[1024,768]{1,0:T(8,128)(2,1)} fusion(bf16[1024,1024]{1,0:T(8,128)(2,1)S(1)} %bitcast.27, bf16[1024,768]{1,0:T(8,128)(2,1)} %bitcast.30), kind=kOutput, calls=%fused_computation.5 | convolution fusion | flops 1611399168 | bytes 5242880 | tf_op jit(solution)/shard_map/dot_general | solution.py:50
  189.4 32.4 %all-to-all-done.3 = bf16[8,128,768]{2,1,0:T(8,128)(2,1)} async-done(((bf16[8,128,768]{2,1,0:T(8,128)(2,1)}), bf16[8,128,768]{2,1,0:T(8,128)(2,1)}, u32[]{:S(2)}, u32[]{:S(2)}) %all-to-all-start.3) | async-done | bytes 1572896 | tf_op jit(solution)/shard_map/all_to_all | solution.py:43
  221.7 4.4 %convolution_convert_fusion.2 = bf16[1024,768]{1,0:T(8,128)(2,1)} fusion(bf16[1024,1024]{1,0:T(8,128)(2,1)S(1)} %bitcast.28, bf16[1024,768]{1,0:T(8,128)(2,1)} %bitcast.10), kind=kOutput, calls=%fused_computation.4 | convolution fusion | flops 1611399168 | bytes 5242880 | tf_op jit(solution)/shard_map/dot_general | solution.py:50
  227.0 2.4 subtract_convert_fusion.1
  229.4 2.1 collective-permute-start
  233.4 2.2 collective-permute-done
  236.3 3.2 %constant_dynamic-update-slice_fusion.2 = (bf16[256,4352]{1,0:T(8,128)(2,1)}, bf16[256,896]{1,0:T(8,128)(2,1)S(1)}, f32[256,896]{1,0:T(8,128)S(1)}) fusion(bf16[256,4352]{1,0:T(8,128)(2,1)} %constant_dynamic-update-slice_fusion.3, f32[256,3328]{1,0:T(8,128)} %param.9, f32[]{:T(128)} %bitcast.7, bf16[256,3328]{1,0:T(8,128)(2,1)} %param.11, f32[]{:T(128)} %bitcast.6, ...), kind=kLoop, calls=%fused_computation.56 | loop fusion | flops 4358144 | bytes 4129792
  239.5 1.9 collective-permute-start.1
  241.5 3.0 %fusion.32 = (bf16[256,4352]{1,0:T(8,128)(2,1)}, f32[256,768]{1,0:T(8,128)S(1)}) fusion(bf16[256,4352]{1,0:T(8,128)(2,1)} %get-tuple-element.8, f32[256,3328]{1,0:T(8,128)} %param.9, f32[]{:T(128)} %bitcast.7, bf16[256,3328]{1,0:T(8,128)(2,1)} %param.11, f32[]{:T(128)} %bitcast.6, bf16[256,768]{1,0:T(8,128)(2,1)} %reduce-scatter.7.cloned.1.call-done, ...), kind=kLoop, calls=%fused_computation.50 | loop fusion | flops 3735552 | bytes 3146752
  244.4 6.5 %reduce-scatter.9.cloned.1.call-done = bf16[256,768]{1,0:T(8,128)(2,1)} async-done(((bf16[1024,768]{1,0:T(8,128)(2,1)}), bf16[256,768]{1,0:T(8,128)(2,1)}) %reduce-scatter.9.cloned.1.call-update) | async-done | bytes 393232 | tf_op jit(solution)/shard_map/reduce_scatter | solution.py:53
  250.9 3.0 %fusion.33 = (bf16[256,4352]{1,0:T(8,128)(2,1)}, f32[256,768]{1,0:T(8,128)S(1)}) fusion(bf16[256,4352]{1,0:T(8,128)(2,1)} %get-tuple-element.6, f32[256,3328]{1,0:T(8,128)} %param.9, f32[]{:T(128)} %bitcast.7, bf16[256,3328]{1,0:T(8,128)(2,1)} %param.11, f32[]{:T(128)} %bitcast.6, bf16[256,768]{1,0:T(8,128)(2,1)} %reduce-scatter.9.cloned.1.call-done, ...), kind=kLoop, calls=%fused_computation.51 | loop fusion | flops 3735552 | bytes 3146752
  253.9 2.0 pad_maximum_fusion
  256.7 2.4 dynamic-slice_select_fusion
  (33 shorter events, 10.5 us)
Async XLA Ops:
  7.2 44.2 %all-gather.2.cloned.1.call-start = ((), (), s32[]{:S(2)}) async-start(), calls=%async_computation.9 | async-start | bytes 2359296 | tf_op jit(solution)/shard_map/all_gather | solution.py:35
  31.0 48.4 %all-to-all-start.4 = ((bf16[8,128,896]{2,1,0:T(8,128)(2,1)}), bf16[8,128,896]{2,1,0:T(8,128)(2,1)}, u32[]{:S(2)}, u32[]{:S(2)}) async-start(bf16[8,128,896]{2,1,0:T(8,128)(2,1)} %stack.11), calls=%async_computation.7 | async-start | bytes 3670016 | tf_op jit(solution)/shard_map/all_to_all | solution.py:43
  80.9 50.4 %all-to-all-start.1 = ((bf16[8,128,896]{2,1,0:T(8,128)(2,1)}), bf16[8,128,896]{2,1,0:T(8,128)(2,1)}, u32[]{:S(2)}, u32[]{:S(2)}) async-start(bf16[8,128,896]{2,1,0:T(8,128)(2,1)} %stack.8), calls=%async_computation.1 | async-start | bytes 3670016 | tf_op jit(solution)/shard_map/all_to_all | solution.py:43
  85.2 141.8 %reduce-scatter.11.cloned.1.call-start = ((), (), s32[]{:S(2)}) async-start(), calls=%async_computation.13 | async-start | bytes 2293760 | tf_op jit(solution)/shard_map/reduce_scatter | solution.py:53
  90.4 145.9 %reduce-scatter.5.cloned.1.call-start = ((), (), s32[]{:S(2)}) async-start(), calls=%async_computation.10 | async-start | bytes 2293760 | tf_op jit(solution)/shard_map/reduce_scatter | solution.py:53
  180.5 41.2 %all-to-all-start.3 = ((bf16[8,128,768]{2,1,0:T(8,128)(2,1)}), bf16[8,128,768]{2,1,0:T(8,128)(2,1)}, u32[]{:S(2)}, u32[]{:S(2)}) async-start(bf16[8,128,768]{2,1,0:T(8,128)(2,1)} %stack.10), calls=%async_computation.5 | async-start | bytes 3145728 | tf_op jit(solution)/shard_map/all_to_all | solution.py:43
  184.8 56.7 %reduce-scatter.7.cloned.1.call-start = ((), (), s32[]{:S(2)}) async-start(), calls=%async_computation.11 | async-start | bytes 1966080 | tf_op jit(solution)/shard_map/reduce_scatter | solution.py:53
  189.3 61.6 %reduce-scatter.9.cloned.1.call-start = ((), (), s32[]{:S(2)}) async-start(), calls=%async_computation.12 | async-start | bytes 1966080 | tf_op jit(solution)/shard_map/reduce_scatter | solution.py:53
  226.2 5.3 %copy-start.1 = (s32[8]{0:T(128)S(1)}, s32[8]{0:T(128)}, u32[]{:S(2)}) copy-start(s32[8]{0:T(128)} %param.12) | copy-start | bytes 100
  229.4 6.3 %collective-permute-start = (bf16[256,256]{1,0:T(8,128)(2,1)S(1)}, bf16[256,256]{1,0:T(8,128)(2,1)S(1)}, u32[]{:S(2)}, u32[]{:S(2)}) collective-permute-start(bf16[256,256]{1,0:T(8,128)(2,1)S(1)} %slice.72), channel_id=1, source_target_pairs={{0,1},{1,2},{2,3},{3,4},{4,5},{5,6},{6,7},{8,9},{9,10},{10,11},{11... | collective-permute-start | bytes 393224 | tf_op jit(solution)/shard_map/ppermute | solution.py:68
  239.5 17.1 %collective-permute-start.1 = (bf16[256,256]{1,0:T(8,128)(2,1)S(1)}, bf16[256,256]{1,0:T(8,128)(2,1)S(1)}, u32[]{:S(2)}, u32[]{:S(2)}) collective-permute-start(bf16[256,256]{1,0:T(8,128)(2,1)S(1)} %slice.73), channel_id=1, source_target_pairs={{1,0},{2,1},{3,2},{4,3},{5,4},{6,5},{7,6},{9,8},{10,9},{11,10},{12... | collective-permute-start | bytes 393224 | tf_op jit(solution)/shard_map/ppermute | solution.py:69
  253.9 2.7 %copy-start = (bf16[256,4352]{1,0:T(8,128)(2,1)S(1)}, bf16[256,4352]{1,0:T(8,128)(2,1)}, u32[]{:S(2)}) copy-start(bf16[256,4352]{1,0:T(8,128)(2,1)} %get-tuple-element.4) | copy-start | bytes 6684676
Sparse Core Ops, SparseCore 0:
  28.6 22.7 all-gather.1
  90.5 31.6 reduce-scatter.10
  136.5 26.4 reduce-scatter.4
  189.4 29.7 reduce-scatter.6
  226.3 24.5 reduce-scatter.8
